TPU v7x, 32 devices: a whole 2x2x4 slice. The times are simulated.
32 devices in a mesh: row: 4 (over y, x), col: 8 (over z, core).
Axes of the slice: x: 2, y: 2, z: 4, core: 2. Of those that a mesh axis runs over, the one named last changes fastest.
Arguments:
- tokens_in: bfloat16 [768, 8192], P('row', 'col'), may hold values from -6 to 6
- grad_out: bfloat16 [768, 8192], P('row', 'col'), may hold values from -1.5 to 1.5
- w_gate: bfloat16 [8192, 28672], P('col', 'row'), may hold values from -0.0625 to 0.0625
- w_up: bfloat16 [8192, 28672], P('col', 'row'), may hold values from -0.0625 to 0.0625
- w_down: bfloat16 [28672, 8192], P('row', 'col'), may hold values from -0.03125 to 0.03125
Outputs:
- grad_input: bfloat16 [768, 8192], P('row', 'col')
- grad_gate: bfloat16 [8192, 28672], P('col', 'row')
- grad_up: bfloat16 [8192, 28672], P('col', 'row')
- grad_down: bfloat16 [28672, 8192], P('row', 'col')
All inputs are finite; a program needn't handle non-finite values.
Results may differ from a plain program's by a relative error of at most 0.023.
Values may be sent and summed in bfloat16 or wider, within the bound.
A program may use at most 256 MiB of HBM per device.

v0:
```python
import functools

import jax
import jax.numpy as jnp
from jax import lax
from jax.experimental import pallas as pl
from jax.experimental.pallas import tpu as pltpu
from jax.sharding import PartitionSpec as P

MESH = pl.DeviceIdType.MESH
CHUNK = 128
SLACK = 2
BF16 = jnp.bfloat16
F32 = jnp.float32


def dot_nt(left, right):
    return lax.dot_general(left, right, (((1,), (1,)), ((), ())), preferred_element_type=F32)


def tile(size, most):
    while size % most:
        most //= 2
    return most


def kernel(
    cfg,
    x_in, g_in, wg_hbm, wu_hbm, wd_hbm,
    gi_ref, gg_hbm, gu_hbm, gd_hbm,
    x_ref, xt_ref, g_ref, wf, wdf, wb, own, pout, prec, rs_in, rs_out, act, acc, hid_t, og, od,
    row_send, row_recv, wf_sem, wb_sem, out_sem,
    p_send, p_recv, rs_send, rs_recv, an_send, an_recv, ap_send, ap_recv, tick,
):
    R, Z, N, C, S1, S2, S3 = cfg
    T, DL = x_ref.shape
    H, Q = T // 2, T // 4
    me = lax.axis_index("col")
    pos = lax.div(me, 2)
    core = lax.rem(me, 2)
    partner = me + 1 - 2 * core
    has_left, has_right = pos > 0, pos < Z - 1
    left = jnp.where(has_left, me - 2, partner)
    right = jnp.where(has_right, me + 2, partner)

    def signal(sem, dev):
        pl.semaphore_signal(sem, inc=1, device_id={"col": dev}, device_id_type=MESH)

    row = lax.axis_index("row")
    TR = x_in.shape[0]
    barrier = pltpu.get_barrier_semaphore()
    for k in range(1, R):
        pl.semaphore_signal(
            barrier, inc=1, device_id={"row": lax.rem(row + k, R)}, device_id_type=MESH
        )
    signal(barrier, partner)

    @pl.when(has_left)
    def _():
        signal(barrier, left)

    @pl.when(has_right)
    def _():
        signal(barrier, right)

    pl.semaphore_wait(barrier, R + jnp.where(has_left, 1, 0) + jnp.where(has_right, 1, 0))

    def remote(src, dst, ssem, rsem, dev):
        return pltpu.make_async_remote_copy(
            src_ref=src, dst_ref=dst, send_sem=ssem, recv_sem=rsem,
            device_id={"col": dev}, device_id_type=MESH,
        )

    def cols(j):
        return pl.ds(pl.multiple_of(j * C, C), C)

    def wf_copies(j):
        s = lax.rem(j, 2)
        return (
            pltpu.make_async_copy(wg_hbm.at[:, cols(j)], wf.at[s, :, pl.ds(0, C)], wf_sem.at[s, 0]),
            pltpu.make_async_copy(wu_hbm.at[:, cols(j)], wf.at[s, :, pl.ds(C, C)], wf_sem.at[s, 1]),
            pltpu.make_async_copy(wd_hbm.at[cols(j), :], wdf.at[s], wf_sem.at[s, 2]),
        )

    def wb_copies(j):
        s = lax.rem(j, 2)
        return (
            pltpu.make_async_copy(wg_hbm.at[:, cols(j)], wb.at[s, :, pl.ds(0, C)], wb_sem.at[s, 0]),
            pltpu.make_async_copy(wu_hbm.at[:, cols(j)], wb.at[s, :, pl.ds(C, C)], wb_sem.at[s, 1]),
        )

    def out_copies(j):
        s = lax.rem(j, 2)
        return (
            pltpu.make_async_copy(og.at[s, :, pl.ds(0, C)], gg_hbm.at[:, cols(j)], out_sem.at[s, 0]),
            pltpu.make_async_copy(og.at[s, :, pl.ds(C, C)], gu_hbm.at[:, cols(j)], out_sem.at[s, 1]),
            pltpu.make_async_copy(od.at[s], gd_hbm.at[cols(j), :], out_sem.at[s, 2]),
        )

    def start(copies):
        for copy in copies:
            copy.start()

    def wait(copies):
        for copy in copies:
            copy.wait()

    def pair_copy(j):
        s1 = lax.rem(j, S1)
        s = lax.rem(j, 2)
        return remote(pout.at[s], prec.at[s1], p_send.at[s], p_recv.at[s1], partner)

    def sum_copy(side, j):
        s = lax.rem(j, S2)
        dev = left if side == 0 else right
        return remote(rs_out.at[side, s], rs_in.at[side, s], rs_send.at[side, s], rs_recv.at[side, s], dev)

    def act_rows(side, which):
        return pl.ds(pl.multiple_of(which * H + side * Q, Q), Q)

    def act_copy(side, j):
        s = lax.rem(j, S3)
        rows = act.at[s, act_rows(side, core), :]
        dev = right if side == 0 else left
        return remote(rows, rows, an_send.at[side, s], an_recv.at[side, s], dev)

    def act_pair_copy(side, j):
        s = lax.rem(j, S3)
        rows = act.at[s, act_rows(side, core), :]
        return remote(rows, rows, ap_send.at[side, s], ap_recv.at[side, s], partner)

    def act_forwards(side):
        return has_right if side == 0 else has_left

    RB = tile(Q, 32)

    def over_rows(side, j, add_in, finish):
        s1, s2, s3 = lax.rem(j, S1), lax.rem(j, S2), lax.rem(j, S3)

        def body(i, carry):
            local = pl.ds(pl.multiple_of(side * Q + i * RB, RB), RB)
            part = pl.ds(pl.multiple_of(i * RB, RB), RB)
            total = own[s1, local, :].astype(F32) + prec[s1, local, :].astype(F32)
            if add_in:
                total = total + rs_in[side, s2, part, :].astype(F32)
            if finish:
                gate, up_val, grad_hidden = total[:, :C], total[:, C : 2 * C], total[:, 2 * C :]
                sig = 1.0 / (1.0 + jnp.exp(-gate))
                dst = pl.ds(pl.multiple_of(core * H + side * Q + i * RB, RB), RB)
                act[s3, dst, pl.ds(0, C)] = (
                    grad_hidden * up_val * sig * (1.0 + gate * (1.0 - sig))
                ).astype(BF16)
                act[s3, dst, pl.ds(C, C)] = (grad_hidden * gate * sig).astype(BF16)
                act[s3, dst, pl.ds(2 * C, C)] = (gate * sig * up_val).astype(BF16)
            else:
                rs_out[side, s2, part, :] = total.astype(BF16)
            return carry

        lax.fori_loop(0, Q // RB, body, 0)

    def sums(t, side):
        order = pos if side == 1 else Z - 1 - pos
        j = t - 1 - order
        live = jnp.logical_and(j >= 0, j < N)

        @pl.when(jnp.logical_and(live, order > 0))
        def _():
            sum_copy(side, j).wait_recv()

        @pl.when(jnp.logical_and(live, order < Z - 1))
        def _():
            @pl.when(j >= S2)
            def _():
                sum_copy(side, j).wait_send()

            @pl.when(order == 0)
            def _():
                over_rows(side, j, False, False)

            @pl.when(order > 0)
            def _():
                over_rows(side, j, True, False)

            sum_copy(side, j).start()

        @pl.when(jnp.logical_and(live, order == Z - 1))
        def _():
            over_rows(side, j, Z > 1, True)

            @pl.when(act_forwards(side))
            def _():
                act_copy(side, j).start()

            act_pair_copy(side, j).start()

    def spread(t, side):
        order = pos if side == 0 else Z - 1 - pos
        j = t - Z - order

        @pl.when(jnp.logical_and(order > 0, jnp.logical_and(j >= 0, j < N)))
        def _():
            act_copy(side, j).wait_recv()

            @pl.when(act_forwards(side))
            def _():
                act_copy(side, j).start()

            act_pair_copy(side, j).start()

    FB = tile(H, 128)

    def forward(j):
        s, s1 = lax.rem(j, 2), lax.rem(j, S1)

        @pl.when(j + 1 < N)
        def _():
            start(wf_copies(j + 1))

        wait(wf_copies(j))

        @pl.when(j >= 2)
        def _():
            pair_copy(j).wait_send()

        def half(base, dst, slot):
            def body(i, carry):
                src = pl.ds(pl.multiple_of(base + i * FB, FB), FB)
                rows = pl.ds(pl.multiple_of(i * FB, FB), FB)
                dst[slot, rows, pl.ds(0, 2 * C)] = jnp.dot(
                    x_ref[src, :], wf[s], preferred_element_type=F32
                ).astype(BF16)
                dst[slot, rows, pl.ds(2 * C, C)] = dot_nt(g_ref[src, :], wdf[s]).astype(BF16)
                return carry

            lax.fori_loop(0, H // FB, body, 0)

        half((1 - core) * H, pout, s)
        pair_copy(j).start()
        half(core * H, own, s1)

    GB = tile(DL, 256)
    AB = tile(T, 256)

    def backward(j):
        s, s3 = lax.rem(j, 2), lax.rem(j, S3)
        for side in range(2):
            act_pair_copy(side, j).wait_recv()
        wait(wb_copies(j))

        @pl.when(j >= 2)
        def _():
            wait(out_copies(j))

        hid_t[...] = act[s3, :, pl.ds(2 * C, C)].T

        def grads(i, carry):
            rows = pl.ds(pl.multiple_of(i * GB, GB), GB)
            og[s, rows, :] = jnp.dot(
                xt_ref[rows, :], act[s3, :, pl.ds(0, 2 * C)], preferred_element_type=F32
            ).astype(BF16)
            od[s, :, rows] = jnp.dot(
                hid_t[...], g_ref[:, rows], preferred_element_type=F32
            ).astype(BF16)
            return carry

        lax.fori_loop(0, DL // GB, grads, 0)
        start(out_copies(j))

        def inputs(i, carry):
            rows = pl.ds(pl.multiple_of(i * AB, AB), AB)
            acc[rows, :] += dot_nt(act[s3, rows, pl.ds(0, 2 * C)], wb[s])
            return carry

        lax.fori_loop(0, T // AB, inputs, 0)
        for side in range(2):
            @pl.when(act_forwards(side))
            def _():
                act_copy(side, j).wait_send()

            act_pair_copy(side, j).wait_send()

    def tick_wait():
        @pl.when(has_left)
        def _():
            pl.semaphore_wait(tick.at[0], 1)

        @pl.when(has_right)
        def _():
            pl.semaphore_wait(tick.at[1], 1)

        pl.semaphore_wait(tick.at[2], 1)

    def row_copy(which, k, owner):
        src, dst = ((x_in, x_ref), (g_in, g_ref))[which]
        rows = pl.ds(pl.multiple_of(owner * TR, TR), TR)
        return pltpu.make_async_remote_copy(
            src_ref=src, dst_ref=dst.at[rows, :],
            send_sem=row_send.at[which, k], recv_sem=row_recv.at[which, k],
            device_id={"row": lax.rem(row + k, R)}, device_id_type=MESH,
        )

    for which in range(2):
        for k in range(1, R):
            row_copy(which, k, row).start()
    start(wf_copies(0))
    mine = pl.ds(pl.multiple_of(row * TR, TR), TR)
    x_ref[mine, :] = x_in[...]
    g_ref[mine, :] = g_in[...]
    acc[...] = jnp.zeros_like(acc)
    steps = N + 2 * Z
    for k in range(1, R):
        row_copy(0, k, lax.rem(row - k + R, R)).wait_recv()

    def turn(i, carry):
        rows = pl.ds(pl.multiple_of(i * GB, GB), GB)
        xt_ref[rows, :] = x_ref[:, rows].T
        return carry

    lax.fori_loop(0, DL // GB, turn, 0)
    for k in range(1, R):
        row_copy(1, k, lax.rem(row - k + R, R)).wait_recv()

    def step(t, carry):
        @pl.when(t >= SLACK)
        def _():
            tick_wait()

        nxt = t + 1 - 2 * Z

        @pl.when(jnp.logical_and(nxt >= 0, nxt < N))
        def _():
            start(wb_copies(nxt))

        @pl.when(jnp.logical_and(t >= 1, t - 1 < N))
        def _():
            pair_copy(t - 1).wait_recv()

        sums(t, 0)
        sums(t, 1)

        @pl.when(t < N)
        def _():
            forward(t)

        spread(t, 0)
        spread(t, 1)

        @pl.when(t >= 2 * Z)
        def _():
            backward(t - 2 * Z)

        signal(tick.at[2], partner)

        @pl.when(has_left)
        def _():
            signal(tick.at[1], left)

        @pl.when(has_right)
        def _():
            signal(tick.at[0], right)

        return carry

    lax.fori_loop(0, steps, step, 0)
    for _ in range(SLACK):
        tick_wait()
    for which in range(2):
        for k in range(1, R):
            row_copy(which, k, row).wait_send()
    for j in range(max(N - 2, 0), N):
        pair_copy(j).wait_send()
        wait(out_copies(j))
    for side in range(2):
        @pl.when(has_left if side == 0 else has_right)
        def _():
            for j in range(max(N - S2, 0), N):
                sum_copy(side, j).wait_send()

    gi_ref[...] = acc[...].astype(BF16)


def fused(n_row, n_col, x, g, wg, wu, wd):
    T, DL = x.shape[0] * n_row, x.shape[1]
    F = wg.shape[1]
    C = CHUNK
    Z, N = n_col // 2, F // C
    S1, S2, S3 = Z + SLACK, SLACK + 1, Z + SLACK
    H, Q = T // 2, T // 4
    vm = pl.BlockSpec(memory_space=pltpu.VMEM)
    hbm = pl.BlockSpec(memory_space=pl.ANY)
    dma = pltpu.SemaphoreType.DMA
    return pl.pallas_call(
        functools.partial(kernel, (n_row, Z, N, C, S1, S2, S3)),
        out_shape=(
            jax.ShapeDtypeStruct((T, DL), BF16),
            jax.ShapeDtypeStruct((DL, F), BF16),
            jax.ShapeDtypeStruct((DL, F), BF16),
            jax.ShapeDtypeStruct((F, DL), BF16),
        ),
        in_specs=[vm, vm, hbm, hbm, hbm],
        out_specs=(vm, hbm, hbm, hbm),
        scratch_shapes=[
            pltpu.VMEM((T, DL), BF16),
            pltpu.VMEM((DL, T), BF16),
            pltpu.VMEM((T, DL), BF16),
            pltpu.VMEM((2, DL, 2 * C), BF16),
            pltpu.VMEM((2, C, DL), BF16),
            pltpu.VMEM((2, DL, 2 * C), BF16),
            pltpu.VMEM((S1, H, 3 * C), BF16),
            pltpu.VMEM((2, H, 3 * C), BF16),
            pltpu.VMEM((S1, H, 3 * C), BF16),
            pltpu.VMEM((2, S2, Q, 3 * C), BF16),
            pltpu.VMEM((2, S2, Q, 3 * C), BF16),
            pltpu.VMEM((S3, T, 3 * C), BF16),
            pltpu.VMEM((T, DL), F32),
            pltpu.VMEM((C, T), BF16),
            pltpu.VMEM((2, DL, 2 * C), BF16),
            pltpu.VMEM((2, C, DL), BF16),
            dma((2, n_row)), dma((2, n_row)),
            dma((2, 3)), dma((2, 2)), dma((2, 3)),
            dma((2,)), dma((S1,)),
            dma((2, S2)), dma((2, S2)),
            dma((2, S3)), dma((2, S3)),
            dma((2, S3)), dma((2, S3)),
            pltpu.SemaphoreType.REGULAR((3,)),
        ],
        compiler_params=pltpu.CompilerParams(
            collective_id=0, has_side_effects=True, vmem_limit_bytes=60 * 1024 * 1024
        ),
    )(x, g, wg, wu, wd)


def move(a_in, b_in, c_in, a_out, b_out, c_out):
    a_out[...] = a_in[...]
    b_out[...] = b_in[...]
    c_out[...] = c_in[...]


def settle(arrays):
    parts = 16
    specs = [pl.BlockSpec((a.shape[0] // parts, a.shape[1]), lambda i: (i, 0)) for a in arrays]
    size = sum(a.size * a.dtype.itemsize for a in arrays)
    return pl.pallas_call(
        move,
        grid=(parts,),
        out_shape=tuple(jax.ShapeDtypeStruct(a.shape, a.dtype) for a in arrays),
        in_specs=specs,
        out_specs=tuple(specs),
        cost_estimate=pl.CostEstimate(flops=0, bytes_accessed=2 * size, transcendentals=0),
        compiler_params=pltpu.CompilerParams(vmem_limit_bytes=60 * 1024 * 1024),
    )(*arrays)


def solution(mesh):
    n_row, n_col = mesh.shape["row"], mesh.shape["col"]

    def local(tokens_in, grad_out, w_gate, w_up, w_down):
        acc, *grads = fused(n_row, n_col, tokens_in, grad_out, w_gate, w_up, w_down)
        grad_input = lax.psum_scatter(acc, "row", scatter_dimension=0, tiled=True)
        return (grad_input, *settle(grads))

    return jax.shard_map(
        local,
        mesh=mesh,
        in_specs=(
            P("row", "col"),
            P("row", "col"),
            P("col", "row"),
            P("col", "row"),
            P("row", "col"),
        ),
        out_specs=(P("row", "col"), P("col", "row"), P("col", "row"), P("row", "col")),
        check_vma=False,
    )
```

profile of v0, /device:TPU:0, one launch (start us, length us, event | category | flops | bytes accessed | tf_op | source)
XLA Modules:
  0.0 474.2 jit_solution(2215399656226674597)
XLA Ops:
  7.2 0.0 reduce-scatter.2.cloned.1.call-start
  7.2 427.4 %shard_map.84 = (bf16[768,1024]{1,0:T(8,128)(2,1)}, bf16[1024,7168]{1,0:T(8,128)(2,1)}, bf16[1024,7168]{1,0:T(8,128)(2,1)}, bf16[7168,1024]{1,0:T(8,128)(2,1)}) custom-call(bf16[192,1024]{1,0:T(8,128)(2,1)} %x_in.1, bf16[192,1024]{1,0:T(8,128)(2,1)} %g_in.1, bf16[1024,7168]{1,0:T(8,128)(2,1)} %wg_hbm.1, bf16[1024,7168]{1,0:T(8,128)(2,1)} %wu_hbm.1, ...), custom_call_target="tpu_custom_call" | custom-call | tf_op jit(solution)/shard_map/pallas_call | solution.py:392
  434.6 0.0 reduce-scatter.2.cloned.1.call-update
  434.6 32.7 %shard_map.85 = (bf16[1024,7168]{1,0:T(8,128)(2,1)}, bf16[1024,7168]{1,0:T(8,128)(2,1)}, bf16[7168,1024]{1,0:T(8,128)(2,1)}) custom-call(bf16[1024,7168]{1,0:T(8,128)(2,1)} %get-tuple-element.12.a_in, bf16[1024,7168]{1,0:T(8,128)(2,1)} %get-tuple-element.13.b_in, bf16[7168,1024]{1,0:T(8,128)(2,1)} %get-tuple-element.14.c_in), custom_call_target="tpu_custom_call" | custom-call | bytes 88080384 | tf_op jit(solution)/shard_map/pallas_call | solution.py:443
  467.4 0.0 reduce-scatter.2.cloned.1.call-done
Async XLA Ops:
  7.2 460.2 %reduce-scatter.2.cloned.1.call-start = ((), (), s32[]{:S(2)}) async-start(), calls=%async_computation.1 | async-start | bytes 1966080 | tf_op jit(solution)/shard_map/reduce_scatter | solution.py:459
Sparse Core Ops, SparseCore 0:
  434.7 31.3 reduce-scatter.1
where the time goes:
time: 475 us; the launch traced here: 474 us
  Pallas kernels  460 us (97%)
  between operations  14 us (3%)
    pallas_call x1, Pallas kernels, fused(): pl.pallas_call(functools.partial(kernel, (n_row, Z, N, C, S1, S2, S3)), o...  427 us
    pallas_call x1, Pallas kernels, settle(): pl.pallas_call(move, grid=(parts,), out_shape=tuple((jax.ShapeDtypeStruct...  32.7 us
  transfers between devices with their start and end apart: 1, of which 0 were waited for; matrix products, arithmetic and copies ran while one was open for 0% of the time, Pallas kernels for 7%

commit v1 on v0

v1 whole, which is shorter than its diff:
```python
import functools

import jax
import jax.numpy as jnp
from jax import lax
from jax.experimental import pallas as pl
from jax.experimental.pallas import tpu as pltpu
from jax.sharding import PartitionSpec as P

MESH = pl.DeviceIdType.MESH
CHUNK = 512
EARLY = 4
GROUPS = 4
SLACK = 2
BF16 = jnp.bfloat16
F32 = jnp.float32


def dot_nt(left, right):
    return lax.dot_general(left, right, (((1,), (1,)), ((), ())), preferred_element_type=F32)


def tile(size, most):
    while size % most:
        most //= 2
    return most


def kernel(
    cfg,
    x_in, g_in, wg_hbm, wu_hbm, wd_hbm,
    gi_ref, gg_hbm, gu_hbm, gd_hbm,
    x_ref, xt_ref, g_ref, wf, wdf, wb, part, prec, rs_in, rs_out, act, acc, hid_t, og, od,
    row_send, row_recv, wf_sem, wb_sem, out_sem,
    p_send, p_recv, rs_send, rs_recv, an_send, an_recv, ap_send, ap_recv, tick,
):
    R, Z, NC, C, K, S1, S2, S3 = cfg
    T, DL = x_ref.shape
    N = NC * GROUPS
    G = T // GROUPS
    H, Q = G // 2, G // 4
    RPG = R // GROUPS
    me = lax.axis_index("col")
    pos = lax.div(me, 2)
    core = lax.rem(me, 2)
    partner = me + 1 - 2 * core
    has_left, has_right = pos > 0, pos < Z - 1
    left = jnp.where(has_left, me - 2, partner)
    right = jnp.where(has_right, me + 2, partner)

    def signal(sem, dev):
        pl.semaphore_signal(sem, inc=1, device_id={"col": dev}, device_id_type=MESH)

    row = lax.axis_index("row")
    TR = x_in.shape[0]
    barrier = pltpu.get_barrier_semaphore()
    for k in range(1, R):
        pl.semaphore_signal(
            barrier, inc=1, device_id={"row": lax.rem(row + k, R)}, device_id_type=MESH
        )
    signal(barrier, partner)

    @pl.when(has_left)
    def _():
        signal(barrier, left)

    @pl.when(has_right)
    def _():
        signal(barrier, right)

    pl.semaphore_wait(barrier, R + jnp.where(has_left, 1, 0) + jnp.where(has_right, 1, 0))

    def block(j):
        early = lax.div(jnp.maximum(j - K, 0), GROUPS - 1)
        return jnp.where(j < K, j, jnp.where(j < K * GROUPS, early, lax.div(j, GROUPS)))

    def group(j):
        early = 1 + lax.rem(jnp.maximum(j - K, 0), GROUPS - 1)
        k = jnp.where(j < K, 0, jnp.where(j < K * GROUPS, early, lax.rem(j, GROUPS)))
        mine = lax.div(row, RPG)
        total, bit = 0, 1
        while bit < GROUPS:
            total = total + bit * lax.rem(lax.div(mine, bit) + lax.div(k, bit), 2)
            bit *= 2
        return total

    def load(j):
        return jnp.where(j < K, j, K + block(j))

    def load_block(n):
        return jnp.where(n < K, n, n - K)

    def fresh(j):
        later = lax.rem(jnp.maximum(j - K, 0), GROUPS - 1) == 0
        return jnp.logical_or(
            j < K,
            jnp.where(j < K * GROUPS, later, lax.rem(j, GROUPS) == 0),
        )

    def peer(k):
        total, bit = 0, 1
        while bit < R:
            total = total + bit * lax.rem(lax.div(row, bit) + (k // bit) % 2, 2)
            bit *= 2
        return total

    def remote(src, dst, ssem, rsem, dev):
        return pltpu.make_async_remote_copy(
            src_ref=src, dst_ref=dst, send_sem=ssem, recv_sem=rsem,
            device_id={"col": dev}, device_id_type=MESH,
        )

    def cols(c):
        return pl.ds(pl.multiple_of(c * C, C), C)

    def wf_copies(n):
        s, c = lax.rem(n, 2), load_block(n)
        return (
            pltpu.make_async_copy(wg_hbm.at[:, cols(c)], wf.at[s, :, pl.ds(0, C)], wf_sem.at[s, 0]),
            pltpu.make_async_copy(wu_hbm.at[:, cols(c)], wf.at[s, :, pl.ds(C, C)], wf_sem.at[s, 1]),
            pltpu.make_async_copy(wd_hbm.at[cols(c), :], wdf.at[s], wf_sem.at[s, 2]),
        )

    def wb_copies(n):
        s, c = lax.rem(n, 2), load_block(n)
        return (
            pltpu.make_async_copy(wg_hbm.at[:, cols(c)], wb.at[s, :, pl.ds(0, C)], wb_sem.at[s, 0]),
            pltpu.make_async_copy(wu_hbm.at[:, cols(c)], wb.at[s, :, pl.ds(C, C)], wb_sem.at[s, 1]),
        )

    DH, CH = DL // GROUPS, C // GROUPS

    def out_copies(u):
        c, q, h = lax.div(u, GROUPS), lax.rem(u, GROUPS), lax.rem(u, 2)
        rows = pl.ds(pl.multiple_of(q * DH, DH), DH)
        units = pl.ds(pl.multiple_of(c * C + q * CH, CH), CH)
        return (
            pltpu.make_async_copy(og.at[h, :, pl.ds(0, C)], gg_hbm.at[rows, cols(c)], out_sem.at[h, 0]),
            pltpu.make_async_copy(og.at[h, :, pl.ds(C, C)], gu_hbm.at[rows, cols(c)], out_sem.at[h, 1]),
            pltpu.make_async_copy(od.at[h], gd_hbm.at[units, :], out_sem.at[h, 2]),
        )

    def start(copies):
        for copy in copies:
            copy.start()

    def wait(copies):
        for copy in copies:
            copy.wait()

    def half_rows(which):
        return pl.ds(pl.multiple_of(which * H, H), H)

    def pair_copy(j):
        s1 = lax.rem(j, S1)
        s = lax.rem(j, 2)
        return remote(
            part.at[s1, half_rows(1 - core), :], prec.at[s1], p_send.at[s], p_recv.at[s1], partner
        )

    def sum_copy(side, j):
        s = lax.rem(j, S2)
        dev = left if side == 0 else right
        return remote(rs_out.at[side, s], rs_in.at[side, s], rs_send.at[side, s], rs_recv.at[side, s], dev)

    def act_part(side, j):
        rows = pl.ds(pl.multiple_of(group(j) * G + core * H + side * Q, Q), Q)
        return act.at[lax.rem(block(j), S3), rows, :]

    def act_copy(side, j):
        s = lax.rem(j, S1)
        rows = act_part(side, j)
        dev = right if side == 0 else left
        return remote(rows, rows, an_send.at[side, s], an_recv.at[side, s], dev)

    def act_pair_copy(side, j):
        s = lax.rem(j, S1)
        rows = act_part(side, j)
        return remote(rows, rows, ap_send.at[side, s], ap_recv.at[side, s], partner)

    def act_forwards(side):
        return has_right if side == 0 else has_left

    RB = 16 if Q % 16 == 0 else Q

    def over_rows(side, j, add_in, finish):
        s1, s2, s3 = lax.rem(j, S1), lax.rem(j, S2), lax.rem(block(j), S3)
        first = group(j) * G + core * H + side * Q

        def body(i, carry):
            mine = pl.ds(pl.multiple_of(core * H + side * Q + i * RB, RB), RB)
            local = pl.ds(pl.multiple_of(side * Q + i * RB, RB), RB)
            piece = pl.ds(pl.multiple_of(i * RB, RB), RB)

            def total(n):
                at = pl.ds(n * C, C)
                value = part[s1, mine, at].astype(F32) + prec[s1, local, at].astype(F32)
                if add_in:
                    value = value + rs_in[side, s2, piece, at].astype(F32)
                return value

            if finish:
                gate, up_val, grad_hidden = total(0), total(1), total(2)
                sig = 1.0 / (1.0 + jnp.exp(-gate))
                dst = pl.ds(pl.multiple_of(first + i * RB, RB), RB)
                act[s3, dst, pl.ds(0, C)] = (
                    grad_hidden * up_val * sig * (1.0 + gate * (1.0 - sig))
                ).astype(BF16)
                act[s3, dst, pl.ds(C, C)] = (grad_hidden * gate * sig).astype(BF16)
                act[s3, dst, pl.ds(2 * C, C)] = (gate * sig * up_val).astype(BF16)
            else:
                for n in range(3):
                    rs_out[side, s2, piece, pl.ds(n * C, C)] = total(n).astype(BF16)
            return carry

        lax.fori_loop(0, Q // RB, body, 0)

    def sums(t, side):
        order = pos if side == 1 else Z - 1 - pos
        j = t - 1 - order
        live = jnp.logical_and(j >= 0, j < N)

        @pl.when(jnp.logical_and(live, order > 0))
        def _():
            sum_copy(side, j).wait_recv()

        @pl.when(jnp.logical_and(live, order < Z - 1))
        def _():
            @pl.when(j >= S2)
            def _():
                sum_copy(side, j).wait_send()

            @pl.when(order == 0)
            def _():
                over_rows(side, j, False, False)

            @pl.when(order > 0)
            def _():
                over_rows(side, j, True, False)

            sum_copy(side, j).start()

        @pl.when(jnp.logical_and(live, order == Z - 1))
        def _():
            over_rows(side, j, Z > 1, True)

            @pl.when(act_forwards(side))
            def _():
                act_copy(side, j).start()

            act_pair_copy(side, j).start()

    def spread(t, side):
        order = pos if side == 0 else Z - 1 - pos
        j = t - Z - order

        @pl.when(jnp.logical_and(order > 0, jnp.logical_and(j >= 0, j < N)))
        def _():
            act_copy(side, j).wait_recv()

            @pl.when(act_forwards(side))
            def _():
                act_copy(side, j).start()

            act_pair_copy(side, j).start()

    NB = tile(C, 256)
    GB = tile(DH, 256)
    AB = tile(DL, 256)

    def forward(j):
        n, s1 = load(j), lax.rem(j, S1)
        s = lax.rem(n, 2)

        @pl.when(jnp.logical_and(j + 1 < N, fresh(j + 1)))
        def _():
            start(wf_copies(load(j + 1)))

        @pl.when(fresh(j))
        def _():
            wait(wf_copies(n))

        for k in range(1, GROUPS):
            @pl.when(j == K + k - 1)
            def _():
                for m in range(k * RPG, (k + 1) * RPG):
                    row_copy(0, m, peer(m)).wait_recv()
                    row_copy(1, m, peer(m)).wait_recv()

        @pl.when(j >= 2)
        def _():
            pair_copy(j).wait_send()

        src = pl.ds(pl.multiple_of(group(j) * G, G), G)

        def up(i, carry):
            at = pl.ds(pl.multiple_of(i * NB, NB), NB)
            part[s1, :, at] = jnp.dot(
                x_ref[src, :], wf[s, :, at], preferred_element_type=F32
            ).astype(BF16)
            return carry

        lax.fori_loop(0, 2 * C // NB, up, 0)

        def back(i, carry):
            rows = pl.ds(pl.multiple_of(i * NB, NB), NB)
            at = pl.ds(pl.multiple_of(2 * C + i * NB, NB), NB)
            part[s1, :, at] = dot_nt(g_ref[src, :], wdf[s, rows, :]).astype(BF16)
            return carry

        lax.fori_loop(0, C // NB, back, 0)
        pair_copy(j).start()

    def inputs(j):
        s, s3 = lax.rem(load(j), 2), lax.rem(block(j), S3)
        for side in range(2):
            act_pair_copy(side, j).wait_recv()

        @pl.when(fresh(j))
        def _():
            wait(wb_copies(load(j)))

        rows = pl.ds(pl.multiple_of(group(j) * G, G), G)

        def add(i, carry):
            at = pl.ds(pl.multiple_of(i * AB, AB), AB)
            acc[rows, at] += dot_nt(act[s3, rows, pl.ds(0, 2 * C)], wb[s, at, :])
            return carry

        lax.fori_loop(0, DL // AB, add, 0)
        for side in range(2):
            @pl.when(act_forwards(side))
            def _():
                act_copy(side, j).wait_send()

            act_pair_copy(side, j).wait_send()

    def grads(u):
        c, q, h = lax.div(u, GROUPS), lax.rem(u, GROUPS), lax.rem(u, 2)
        s3 = lax.rem(c, S3)

        @pl.when(u >= 2)
        def _():
            wait(out_copies(u))

        @pl.when(c == 0)
        def _():
            def turn(i, carry):
                rows = pl.ds(pl.multiple_of(q * DH + i * GB, GB), GB)
                xt_ref[rows, :] = x_ref[:, rows].T
                return carry

            lax.fori_loop(0, DH // GB, turn, 0)

        hid_t[...] = act[s3, :, pl.ds(pl.multiple_of(2 * C + q * CH, CH), CH)].T

        def weights(i, carry):
            rows = pl.ds(pl.multiple_of(i * GB, GB), GB)
            src = pl.ds(pl.multiple_of(q * DH + i * GB, GB), GB)

            def across(n, carry):
                at = pl.ds(pl.multiple_of(n * NB, NB), NB)
                og[h, rows, at] = jnp.dot(
                    xt_ref[src, :], act[s3, :, at], preferred_element_type=F32
                ).astype(BF16)
                return carry

            return lax.fori_loop(0, 2 * C // NB, across, carry)

        lax.fori_loop(0, DH // GB, weights, 0)

        def down(i, carry):
            at = pl.ds(pl.multiple_of(i * AB, AB), AB)
            od[h, :, at] = jnp.dot(
                hid_t[...], g_ref[:, at], preferred_element_type=F32
            ).astype(BF16)
            return carry

        lax.fori_loop(0, DL // AB, down, 0)
        start(out_copies(u))

    def tick_wait():
        @pl.when(has_left)
        def _():
            pl.semaphore_wait(tick.at[0], 1)

        @pl.when(has_right)
        def _():
            pl.semaphore_wait(tick.at[1], 1)

        pl.semaphore_wait(tick.at[2], 1)

    def row_copy(which, k, owner):
        src, dst = ((x_in, x_ref), (g_in, g_ref))[which]
        rows = pl.ds(pl.multiple_of(owner * TR, TR), TR)
        return pltpu.make_async_remote_copy(
            src_ref=src, dst_ref=dst.at[rows, :],
            send_sem=row_send.at[which, k], recv_sem=row_recv.at[which, k],
            device_id={"row": peer(k)}, device_id_type=MESH,
        )

    for k in range(1, R):
        for which in range(2):
            row_copy(which, k, row).start()
    start(wf_copies(0))
    mine = pl.ds(pl.multiple_of(row * TR, TR), TR)
    x_ref[mine, :] = x_in[...]
    g_ref[mine, :] = g_in[...]
    acc[...] = jnp.zeros_like(acc)
    steps = N + 2 * Z + 1
    for k in range(1, RPG):
        for which in range(2):
            row_copy(which, k, peer(k)).wait_recv()

    def step(t, carry):
        @pl.when(t >= SLACK)
        def _():
            tick_wait()

        nxt = t + 1 - 2 * Z

        @pl.when(jnp.logical_and(jnp.logical_and(nxt >= 0, nxt < N), fresh(nxt)))
        def _():
            start(wb_copies(load(nxt)))

        @pl.when(jnp.logical_and(t >= 1, t - 1 < N))
        def _():
            pair_copy(t - 1).wait_recv()

        sums(t, 0)
        sums(t, 1)

        @pl.when(t < N)
        def _():
            forward(t)

        spread(t, 0)
        spread(t, 1)
        b = t - 2 * Z

        @pl.when(jnp.logical_and(b >= 0, b < N))
        def _():
            inputs(b)

        late = jnp.maximum(b - (N - GROUPS), 0)
        u = jnp.minimum(b, N - GROUPS) - (K + 2) + 2 * late
        more = jnp.where(b >= N - GROUPS, 2, 1)

        def quarter(i, carry):
            grads(u + i)
            return carry

        @pl.when(u >= 0)
        def _():
            lax.fori_loop(0, more, quarter, 0)

        signal(tick.at[2], partner)

        @pl.when(has_left)
        def _():
            signal(tick.at[1], left)

        @pl.when(has_right)
        def _():
            signal(tick.at[0], right)

        return carry

    lax.fori_loop(0, steps, step, 0)
    for _ in range(SLACK):
        tick_wait()
    for which in range(2):
        for k in range(1, R):
            row_copy(which, k, row).wait_send()
    for j in range(max(N - 2, 0), N):
        pair_copy(j).wait_send()
    for u in range(N - 2, N):
        wait(out_copies(u))
    for side in range(2):
        @pl.when(has_left if side == 0 else has_right)
        def _():
            for j in range(max(N - S2, 0), N):
                sum_copy(side, j).wait_send()

    gi_ref[...] = acc[...].astype(BF16)


def fused(n_row, n_col, x, g, wg, wu, wd):
    T, DL = x.shape[0] * n_row, x.shape[1]
    F = wg.shape[1]
    C = tile(F, CHUNK)
    Z, NC = n_col // 2, F // C
    K = EARLY
    S1, S2 = Z + SLACK, SLACK + 1
    S3 = max(K, -(-(Z + K + GROUPS + 1 + SLACK) // GROUPS))
    G = T // GROUPS
    H, Q = G // 2, G // 4
    vm = pl.BlockSpec(memory_space=pltpu.VMEM)
    hbm = pl.BlockSpec(memory_space=pl.ANY)
    dma = pltpu.SemaphoreType.DMA
    return pl.pallas_call(
        functools.partial(kernel, (n_row, Z, NC, C, K, S1, S2, S3)),
        out_shape=(
            jax.ShapeDtypeStruct((T, DL), BF16),
            jax.ShapeDtypeStruct((DL, F), BF16),
            jax.ShapeDtypeStruct((DL, F), BF16),
            jax.ShapeDtypeStruct((F, DL), BF16),
        ),
        in_specs=[vm, vm, hbm, hbm, hbm],
        out_specs=(vm, hbm, hbm, hbm),
        scratch_shapes=[
            pltpu.VMEM((T, DL), BF16),
            pltpu.VMEM((DL, T), BF16),
            pltpu.VMEM((T, DL), BF16),
            pltpu.VMEM((2, DL, 2 * C), BF16),
            pltpu.VMEM((2, C, DL), BF16),
            pltpu.VMEM((2, DL, 2 * C), BF16),
            pltpu.VMEM((S1, G, 3 * C), BF16),
            pltpu.VMEM((S1, H, 3 * C), BF16),
            pltpu.VMEM((2, S2, Q, 3 * C), BF16),
            pltpu.VMEM((2, S2, Q, 3 * C), BF16),
            pltpu.VMEM((S3, T, 3 * C), BF16),
            pltpu.VMEM((T, DL), F32),
            pltpu.VMEM((C // GROUPS, T), BF16),
            pltpu.VMEM((2, DL // GROUPS, 2 * C), BF16),
            pltpu.VMEM((2, C // GROUPS, DL), BF16),
            dma((2, n_row)), dma((2, n_row)),
            dma((2, 3)), dma((2, 2)), dma((2, 3)),
            dma((2,)), dma((S1,)),
            dma((2, S2)), dma((2, S2)),
            dma((2, S1)), dma((2, S1)),
            dma((2, S1)), dma((2, S1)),
            pltpu.SemaphoreType.REGULAR((3,)),
        ],
        compiler_params=pltpu.CompilerParams(
            collective_id=0, has_side_effects=True, vmem_limit_bytes=60 * 1024 * 1024
        ),
    )(x, g, wg, wu, wd)


def move(a_in, b_in, c_in, a_out, b_out, c_out):
    a_out[...] = a_in[...]
    b_out[...] = b_in[...]
    c_out[...] = c_in[...]


def settle(arrays):
    parts = 8
    specs = [pl.BlockSpec((a.shape[0] // parts, a.shape[1]), lambda i: (i, 0)) for a in arrays]
    size = sum(a.size * a.dtype.itemsize for a in arrays)
    return pl.pallas_call(
        move,
        grid=(parts,),
        out_shape=tuple(jax.ShapeDtypeStruct(a.shape, a.dtype) for a in arrays),
        in_specs=specs,
        out_specs=tuple(specs),
        cost_estimate=pl.CostEstimate(flops=0, bytes_accessed=2 * size, transcendentals=0),
        compiler_params=pltpu.CompilerParams(vmem_limit_bytes=60 * 1024 * 1024),
    )(*arrays)


def solution(mesh):
    n_row, n_col = mesh.shape["row"], mesh.shape["col"]

    def local(tokens_in, grad_out, w_gate, w_up, w_down):
        acc, *grads = fused(n_row, n_col, tokens_in, grad_out, w_gate, w_up, w_down)
        grad_input = lax.psum_scatter(acc, "row", scatter_dimension=0, tiled=True)
        return (grad_input, *settle(grads))

    return jax.shard_map(
        local,
        mesh=mesh,
        in_specs=(
            P("row", "col"),
            P("row", "col"),
            P("col", "row"),
            P("col", "row"),
            P("row", "col"),
        ),
        out_specs=(P("row", "col"), P("col", "row"), P("col", "row"), P("row", "col")),
        check_vma=False,
    )
```

time: 475 us -> 456 us (0.960)
  Pallas kernels: 460 us -> 442 us
    pallas_call x1, Pallas kernels: 427 us -> 413 us  [fused(): pl.pallas_call(functools.partial(kernel, (n_row, Z, NC, C, K, S1, S2, S3)...]
  transfers between devices with their start and end apart: 1 -> 1, of which waited for: 0 -> 0; matrix products, arithmetic and copies ran while one was open for 0% -> 0% of each run, Pallas kernels for 7% -> 6%
where the time goes in v1:
time: 456 us
  Pallas kernels  442 us (97%)
  between operations  14 us (3%)
    pallas_call x1, Pallas kernels, fused(): pl.pallas_call(functools.partial(kernel, (n_row, Z, NC, C, K, S1, S2, S3)...  413 us
    pallas_call x1, Pallas kernels, settle(): pl.pallas_call(move, grid=(parts,), out_shape=tuple((jax.ShapeDtypeStruct...  28.8 us
  transfers between devices with their start and end apart: 1, of which 0 were waited for; matrix products, arithmetic and copies ran while one was open for 0% of the time, Pallas kernels for 6%

profile of v1, /device:TPU:0, one launch (start us, length us, event | category | flops | bytes accessed | tf_op | source)
XLA Modules:
  0.0 456.3 jit_solution(2326322590626653397)
XLA Ops:
  7.2 0.0 reduce-scatter.2.cloned.1.call-start
  7.2 413.4 %shard_map.84 = (bf16[768,1024]{1,0:T(8,128)(2,1)}, bf16[1024,7168]{1,0:T(8,128)(2,1)}, bf16[1024,7168]{1,0:T(8,128)(2,1)}, bf16[7168,1024]{1,0:T(8,128)(2,1)}) custom-call(bf16[192,1024]{1,0:T(8,128)(2,1)} %x_in.1, bf16[192,1024]{1,0:T(8,128)(2,1)} %g_in.1, bf16[1024,7168]{1,0:T(8,128)(2,1)} %wg_hbm.1, bf16[1024,7168]{1,0:T(8,128)(2,1)} %wu_hbm.1, ...), custom_call_target="tpu_custom_call" | custom-call | tf_op jit(solution)/shard_map/pallas_call | solution.py:501
  420.6 0.0 reduce-scatter.2.cloned.1.call-update
  420.6 28.8 %shard_map.85 = (bf16[1024,7168]{1,0:T(8,128)(2,1)}, bf16[1024,7168]{1,0:T(8,128)(2,1)}, bf16[7168,1024]{1,0:T(8,128)(2,1)}) custom-call(bf16[1024,7168]{1,0:T(8,128)(2,1)} %get-tuple-element.12.a_in, bf16[1024,7168]{1,0:T(8,128)(2,1)} %get-tuple-element.13.b_in, bf16[7168,1024]{1,0:T(8,128)(2,1)} %get-tuple-element.14.c_in), custom_call_target="tpu_custom_call" | custom-call | bytes 88080384 | tf_op jit(solution)/shard_map/pallas_call | solution.py:551
  449.4 0.0 reduce-scatter.2.cloned.1.call-done
Async XLA Ops:
  7.2 442.3 %reduce-scatter.2.cloned.1.call-start = ((), (), s32[]{:S(2)}) async-start(), calls=%async_computation.1 | async-start | bytes 1966080 | tf_op jit(solution)/shard_map/reduce_scatter | solution.py:567
Sparse Core Ops, SparseCore 0:
  420.8 28.0 reduce-scatter.1

commit v2 on v1

--- a/solution.py
+++ b/solution.py
@@ -300,7 +300,7 @@
             ).astype(BF16)
             return carry
 
-        lax.fori_loop(0, 2 * C // NB, up, 0)
+        lax.fori_loop(0, 2 * C // NB, up, 0, unroll=True)
 
         def back(i, carry):
             rows = pl.ds(pl.multiple_of(i * NB, NB), NB)
@@ -308,7 +308,7 @@
             part[s1, :, at] = dot_nt(g_ref[src, :], wdf[s, rows, :]).astype(BF16)
             return carry
 
-        lax.fori_loop(0, C // NB, back, 0)
+        lax.fori_loop(0, C // NB, back, 0, unroll=True)
         pair_copy(j).start()
 
     def inputs(j):
@@ -327,7 +327,7 @@
             acc[rows, at] += dot_nt(act[s3, rows, pl.ds(0, 2 * C)], wb[s, at, :])
             return carry
 
-        lax.fori_loop(0, DL // AB, add, 0)
+        lax.fori_loop(0, DL // AB, add, 0, unroll=True)
         for side in range(2):
             @pl.when(act_forwards(side))
             def _():
@@ -365,7 +365,7 @@
                 ).astype(BF16)
                 return carry
 
-            return lax.fori_loop(0, 2 * C // NB, across, carry)
+            return lax.fori_loop(0, 2 * C // NB, across, carry, unroll=True)
 
         lax.fori_loop(0, DH // GB, weights, 0)
 
@@ -376,7 +376,7 @@
             ).astype(BF16)
             return carry
 
-        lax.fori_loop(0, DL // AB, down, 0)
+        lax.fori_loop(0, DL // AB, down, 0, unroll=True)
         start(out_copies(u))
 
     def tick_wait():

time: 456 us -> 440 us (0.965)
  Pallas kernels: 442 us -> 426 us
    pallas_call x1, Pallas kernels: 413 us -> 398 us  [fused(): pl.pallas_call(functools.partial(kernel, (n_row, Z, NC, C, K, S1, S2, S3)...]
  transfers between devices with their start and end apart: 1 -> 1, of which waited for: 0 -> 1; matrix products, arithmetic and copies ran while one was open for 0% -> 0% of each run, Pallas kernels for 6% -> 6%
where the time goes in v2:
time: 440 us
  Pallas kernels  426 us (97%)
  between operations  14 us (3%)
    pallas_call x1, Pallas kernels, fused(): pl.pallas_call(functools.partial(kernel, (n_row, Z, NC, C, K, S1, S2, S3)...  398 us
    pallas_call x1, Pallas kernels, settle(): pl.pallas_call(move, grid=(parts,), out_shape=tuple((jax.ShapeDtypeStruct...  28.5 us
  transfers between devices with their start and end apart: 1, of which 1 were waited for; matrix products, arithmetic and copies ran while one was open for 0% of the time, Pallas kernels for 6%

profile of v2, /device:TPU:0, one launch (start us, length us, event | category | flops | bytes accessed | tf_op | source)
XLA Modules:
  0.0 440.3 jit_solution(4647626112128138758)
XLA Ops:
  7.2 0.0 reduce-scatter.2.cloned.1.call-start
  7.2 397.6 %shard_map.84 = (bf16[768,1024]{1,0:T(8,128)(2,1)}, bf16[1024,7168]{1,0:T(8,128)(2,1)}, bf16[1024,7168]{1,0:T(8,128)(2,1)}, bf16[7168,1024]{1,0:T(8,128)(2,1)}) custom-call(bf16[192,1024]{1,0:T(8,128)(2,1)} %x_in.1, bf16[192,1024]{1,0:T(8,128)(2,1)} %g_in.1, bf16[1024,7168]{1,0:T(8,128)(2,1)} %wg_hbm.1, bf16[1024,7168]{1,0:T(8,128)(2,1)} %wu_hbm.1, ...), custom_call_target="tpu_custom_call" | custom-call | tf_op jit(solution)/shard_map/pallas_call | solution.py:501
  404.8 0.0 reduce-scatter.2.cloned.1.call-update
  404.9 28.5 %shard_map.85 = (bf16[1024,7168]{1,0:T(8,128)(2,1)}, bf16[1024,7168]{1,0:T(8,128)(2,1)}, bf16[7168,1024]{1,0:T(8,128)(2,1)}) custom-call(bf16[1024,7168]{1,0:T(8,128)(2,1)} %get-tuple-element.12.a_in, bf16[1024,7168]{1,0:T(8,128)(2,1)} %get-tuple-element.13.b_in, bf16[7168,1024]{1,0:T(8,128)(2,1)} %get-tuple-element.14.c_in), custom_call_target="tpu_custom_call" | custom-call | bytes 88080384 | tf_op jit(solution)/shard_map/pallas_call | solution.py:551
  433.4 0.1 reduce-scatter.2.cloned.1.call-done
Async XLA Ops:
  7.2 426.3 %reduce-scatter.2.cloned.1.call-start = ((), (), s32[]{:S(2)}) async-start(), calls=%async_computation.1 | async-start | bytes 1966080 | tf_op jit(solution)/shard_map/reduce_scatter | solution.py:567
Sparse Core Ops, SparseCore 0:
  405.0 28.4 reduce-scatter.1
